TPU v7x, 512 devices: a whole 4x4x16 slice. The times are simulated.
512 devices in a mesh: dp: 4 (over x), cand: 32 (over z, core), tensor: 4 (over y).
Axes of the slice: x: 4, y: 4, z: 16, core: 2. Of those that a mesh axis runs over, the one named last changes fastest.
Arguments:
- context: bfloat16 [8, 4096, 3584], P('dp', 'cand', 'tensor'), may hold values from -12 to 12
- residual: bfloat16 [8, 4096, 3584], P('dp', ('cand', 'tensor')), may hold values from -36 to 36
- out_weight: bfloat16 [3584, 3584], P('cand', 'tensor'), may hold values from -0.09375 to 0.09375
- adapter_down: bfloat16 [3584, 16], P('tensor'), may hold values from -0.09375 to 0.09375
- adapter_up_weight: bfloat16 [16, 3584], replicated, may hold values from -1.5 to 1.5
- norm_gain: float32 [3584], replicated, may hold values from 0.5 to 1.5
- score_weight: float32 [3584], replicated, may hold values from -0.09375 to 0.09375
- teacher: bfloat16 [8, 4096, 4096], P('dp', 'cand', 'tensor'), may hold values from 0.019897461 to 0.9765625
- pair_mask: int32 [8, 4096, 4096], P('dp', 'cand', 'tensor'), may hold values from 0 to 1, as said below
- loss_scale: float32 [8], P('dp'), may hold values from 65536 to 262144
Outputs:
- context_grad: bfloat16 [8, 4096, 3584], P('dp', 'cand', 'tensor')
- residual_gradient: bfloat16 [8, 4096, 3584], P('dp', ('cand', 'tensor'))
- down_grad: float32 [3584, 16], P('tensor')
- up_weight_gradient: float32 [16, 3584], P(None, 'tensor')
- pair_loss: float32 [8], P('dp')
Inputs may be any that keep to these rules, and one draw needn't show every extreme that they name: pair_mask holds 0 or 1; with P = 32, every pair (i, j) whose group j // P lies 4096 / (2P) groups after i // P, counted round over the 4096 / P groups, is valid.
All inputs are finite; a program needn't handle non-finite values.
Results may differ from a plain program's by a relative error of at most 0.02.
Values may be sent and summed in bfloat16 or wider, within the bound.
No kernel may reach another device: no remote copies, remote signals or barrier semaphores. Data moves between devices by JAX's collectives and lax.ppermute only.
A program may use at most 64 MiB of HBM per device.

v0:
```python
import jax
import jax.numpy as jnp
from jax import lax
from jax.sharding import PartitionSpec as P

ADAPTER_SCALE = 0.5
epsilon = 1e-06
F32 = jnp.float32
BF16 = jnp.bfloat16


def on_device(
    context,
    residual,
    out_weight,
    adapter_down,
    adapter_up_weight,
    norm_gain,
    score_weight,
    teacher,
    pair_mask,
    loss_scale,
):
    queries, cand_rows, _ = context.shape
    width = residual.shape[2]
    cols = teacher.shape[2]
    tensor_count = lax.axis_size("tensor")
    cand_count = lax.axis_size("cand")
    share = cand_rows // tensor_count
    near = cols // cand_rows
    tensor_index = lax.axis_index("tensor")
    dp_index = lax.axis_index("dp")
    full_weight = lax.all_gather(out_weight, "cand", axis=0, tiled=True)
    low_terms = jnp.einsum("qch,hr->qcr", context, adapter_down, preferred_element_type=F32).astype(
        BF16
    )
    low_all = lax.all_gather(low_terms, "tensor", axis=0)
    adapter_in = jnp.sum(low_all.astype(F32), axis=0).astype(BF16)
    adapter_own = lax.dynamic_slice_in_dim(adapter_in, tensor_index * share, share, 1)
    lifted = jnp.einsum("qcr,rd->qcd", adapter_own, adapter_up_weight, preferred_element_type=F32)
    base = residual.astype(F32) + ADAPTER_SCALE * lifted
    valid = pair_mask.astype(F32)
    target = teacher.astype(F32)
    mask_count = jnp.sum(valid, axis=(1, 2))
    row_known = jnp.sum(valid * target, axis=2)
    col_known = jnp.sum(valid * (1.0 - target), axis=1)
    groups = [[a * near + b for b in range(near)] for a in range(cand_count // near)]
    swap = [
        ((a * near + b) * tensor_count + t, (t * near + b) * tensor_count + a)
        for a in range(cand_count // near)
        for b in range(near)
        for t in range(tensor_count)
    ]
    blocks = jnp.swapaxes(pair_mask.astype(BF16).reshape(queries, cand_rows, near, cand_rows), 1, 2)
    blocks = jnp.swapaxes(blocks, 2, 3)
    blocks = jnp.swapaxes(blocks, 0, 1)
    blocks = lax.all_to_all(blocks, "cand", 0, 0, axis_index_groups=groups, tiled=True)
    blocks = lax.ppermute(blocks, ("cand", "tensor"), swap)
    other_valid = jnp.moveaxis(blocks, 0, 2).reshape(queries, cand_rows, cols)
    col_known = jnp.swapaxes(col_known.reshape(queries, near, cand_rows), 0, 1)
    col_known = lax.all_to_all(col_known, "cand", 0, 0, axis_index_groups=groups, tiled=True)
    col_known = lax.ppermute(jnp.sum(col_known, axis=0), ("cand", "tensor"), swap)
    both = valid + other_valid.astype(F32)
    known = row_known + col_known
    full_weight, adapter_in, base, both, known, mask_count = lax.optimization_barrier(
        (full_weight, adapter_in, base, both, known, mask_count)
    )
    by_owner = jnp.swapaxes(context.reshape(queries, tensor_count, share, context.shape[2]), 0, 1)
    head_terms = jnp.einsum(
        "tqch,dh->tqcd", by_owner, full_weight, preferred_element_type=F32
    ).astype(BF16)
    head_terms = lax.all_to_all(head_terms, "tensor", 0, 0, tiled=True)
    hidden = (base + jnp.sum(head_terms.astype(F32), axis=0)).astype(BF16).astype(F32)
    inv_rms = lax.rsqrt(jnp.mean(hidden * hidden, axis=2) + epsilon)
    gain = norm_gain * score_weight
    dot = jnp.sum(hidden * gain, axis=2)
    scores = dot * inv_rms
    slant = inv_rms * inv_rms * dot / width
    unit = inv_rms[:, :, None] * (gain - hidden * slant[:, :, None])
    unit_sent, unit, scores = lax.optimization_barrier((unit.astype(BF16), unit, scores))
    unit_all = lax.all_gather(unit_sent, "tensor", axis=1, tiled=True)
    message = jnp.concatenate([scores, mask_count[:, None]], axis=1)
    message = lax.all_gather(message, "tensor", axis=0)
    own_scores = jnp.swapaxes(message[:, :, :share], 0, 1).reshape(queries, cand_rows)
    message = jnp.concatenate([own_scores, jnp.sum(message[:, :, share], axis=0)[:, None]], axis=1)
    message = lax.all_gather(message, "cand", axis=0)
    count = jnp.sum(message[:, :, cand_rows], axis=0)
    col_scores = lax.dynamic_slice_in_dim(message, tensor_index * near, near, 0)
    col_scores = jnp.swapaxes(col_scores[:, :, :cand_rows], 0, 1).reshape(queries, cols)
    margin = own_scores[:, :, None] - col_scores[:, None, :]
    raw = jnp.sum(both * jax.nn.sigmoid(margin), axis=2) - known
    total = jnp.sum(valid * (jax.nn.softplus(margin) - target * margin), axis=(1, 2))
    sums = lax.psum(jnp.concatenate([raw, total[:, None]], axis=1), "tensor")
    score_grad = sums[:, :cand_rows] * (loss_scale / count)[:, None]
    own_grad = lax.dynamic_slice_in_dim(score_grad, tensor_index * share, share, 1)
    grad_rows = (own_grad[:, :, None] * unit).astype(BF16)
    adapter_unit = ADAPTER_SCALE * jnp.einsum(
        "qcd,rd->qcr", unit_all, adapter_up_weight, preferred_element_type=F32
    )
    context_unit = jnp.einsum(
        "qcd,dh->qch", unit_all, full_weight, preferred_element_type=F32
    ) + jnp.einsum(
        "qcr,hr->qch", adapter_unit.astype(BF16), adapter_down, preferred_element_type=F32
    )
    context_grad = (score_grad[:, :, None] * context_unit).astype(BF16)
    adapter_back = (score_grad[:, :, None] * adapter_unit).astype(BF16)
    down_local = jnp.einsum("qcr,qch->rh", adapter_back, context, preferred_element_type=F32)
    block = lax.dynamic_slice_in_dim(unit_all, tensor_index * context.shape[2], context.shape[2], 2)
    block = (score_grad[:, :, None] * block.astype(F32)).astype(BF16)
    up_local = ADAPTER_SCALE * jnp.einsum(
        "qcr,qcd->rd", adapter_in, block, preferred_element_type=F32
    )
    slots = jnp.zeros((128,), F32)
    slots = lax.dynamic_update_slice_in_dim(slots, sums[:, cand_rows], dp_index * queries, 0)
    flat = jnp.concatenate([down_local, up_local], axis=0)
    columns = flat.shape[1]
    flat = jnp.concatenate([flat, jnp.broadcast_to(slots, (flat.shape[0], 128))], axis=1)
    pieces = lax.all_to_all(flat, "cand", 0, 0, tiled=True)
    piece = jnp.sum(pieces.reshape(cand_count, -1, flat.shape[1]), axis=0)
    piece = lax.psum(piece, "dp")
    flat = lax.all_gather(piece[:, :columns], "cand", axis=0, tiled=True)
    rank = adapter_down.shape[1]
    down_grad = flat[:rank].T
    up_weight_gradient = flat[rank:]
    loss_sum = lax.dynamic_slice_in_dim(piece[0, columns:], dp_index * queries, queries, 0)
    pair_loss = loss_sum / count
    return (context_grad, grad_rows, down_grad, up_weight_gradient, pair_loss)


def solution(mesh):
    in_specs = (
        P("dp", "cand", "tensor"),
        P("dp", ("cand", "tensor"), None),
        P("cand", "tensor"),
        P("tensor", None),
        P(),
        P(),
        P(),
        P("dp", "cand", "tensor"),
        P("dp", "cand", "tensor"),
        P("dp"),
    )
    out_specs = (
        P("dp", "cand", "tensor"),
        P("dp", ("cand", "tensor"), None),
        P("tensor", None),
        P(None, "tensor"),
        P("dp"),
    )
    return jax.shard_map(
        on_device, mesh=mesh, in_specs=in_specs, out_specs=out_specs, check_vma=False
    )
```

profile of v0, /device:TPU:1, one launch (start us, length us, event | category | flops | bytes accessed | tf_op | source)
XLA Modules:
  0.0 317.1 jit_solution(14492580790109656171)
XLA Ops:
  7.2 0.0 copy-start
  7.2 0.0 all-gather.9.cloned.1.call-start
  7.2 0.7 all-gather.9.cloned.1.call-update
  7.9 1.5 copy.36
  9.5 0.1 convert_element_type.65
  9.6 0.0 copy-start.6
  9.6 0.3 copy.38
  9.8 23.6 %all_to_all.24 = bf16[8,2,128,128]{2,3,1,0:T(8,128)(2,1)S(1)} all-to-all(bf16[8,2,128,128]{2,3,1,0:T(8,128)(2,1)S(1)} %copy.38), channel_id=1, replica_groups={{0,4,8,12,16,20,24,28},{32,36,40,44,48,52,56,60},{64,68,72,76,80,84,88,..., dimensions={0} | all-to-all | bytes 1048576 | tf_op jit(solution)/shard_map/all_to_all | solution.py:57
  33.5 0.9 copy.39
  34.3 1.7 collective-permute-start
  36.0 0.3 copy.40
  36.3 0.0 copy-start.4
  36.3 0.0 copy-start.8
  36.3 0.0 copy-start.7
  36.3 0.0 collective-permute-done
  36.3 2.0 fusion.23
  38.3 4.3 %all-to-all-start.1 = ((f32[8,2,128]{2,1,0:T(2,128)}), f32[8,2,128]{2,1,0:T(2,128)S(1)}, u32[]{:S(2)}, u32[]{:S(2)}) async-start(f32[8,2,128]{2,1,0:T(2,128)} %bitcast.8), calls=%async_computation.1 | async-start | bytes 16384 | tf_op jit(solution)/shard_map/all_to_all | solution.py:61
  42.6 0.0 copy-done.8
  42.6 0.2 convolution_convert_fusion
  42.8 94.4 %all-gather = bf16[8,128,16]{1,2,0:T(8,128)(2,1)S(1)} all-gather(bf16[2,128,16]{1,2,0:T(8,128)(2,1)S(1)} %convolution_convert_fusion), channel_id=2, replica_groups=mesh['dp'=4,'cand'=32,'tensor'=4] {'tensor'}, dimensions={0}, use_global_device_ids=true | all-gather | bytes 40960 | tf_op jit(solution)/shard_map/all_gather | solution.py:37
  137.2 0.0 all-to-all-done.1
  137.3 0.7 collective-permute-start.1
  137.9 0.0 copy-done
  137.9 1.3 fusion.10
  139.2 0.0 collective-permute-done.1
  139.2 11.5 %all-gather.9.cloned.1.call-done = bf16[3584,896]{1,0:T(8,128)(2,1)} async-done(((bf16[112,896]{1,0:T(8,128)(2,1)}), bf16[3584,896]{1,0:T(8,128)(2,1)}) %all-gather.9.cloned.1.call-update) | async-done | bytes 6422544 | tf_op jit(solution)/shard_map/all_gather | solution.py:33
  150.8 6.2 %fusion.7 = bf16[4,2,32,3584]{3,2,1,0:T(8,128)(2,1)} fusion(bf16[3584,896]{1,0:T(8,128)(2,1)} %all-gather.9.cloned.1.call-done, bf16[2,4,32,896]{3,2,1,0:T(8,128)(2,1)S(1)} %bitcast.85), kind=kOutput, calls=%fused_computation.5 | convolution fusion | flops 1645084672 | bytes 8716288 | tf_op jit(solution)/shard_map/tqch,dh->tqcd/dot_general | solution.py:69
  156.9 6.8 %all-to-all-start.2 = ((bf16[4,2,32,3584]{3,2,1,0:T(8,128)(2,1)}), bf16[4,2,32,3584]{3,2,1,0:T(8,128)(2,1)S(1)}, u32[]{:S(2)}, u32[]{:S(2)}) async-start(bf16[4,2,32,3584]{3,2,1,0:T(8,128)(2,1)} %fusion.7), calls=%async_computation.2 | async-start | bytes 3670016 | tf_op jit(solution)/shard_map/all_to_all | solution.py:72
  163.7 0.7 mul.141
  164.4 22.3 %all-to-all-done.2 = bf16[4,2,32,3584]{3,2,1,0:T(8,128)(2,1)S(1)} async-done(((bf16[4,2,32,3584]{3,2,1,0:T(8,128)(2,1)}), bf16[4,2,32,3584]{3,2,1,0:T(8,128)(2,1)S(1)}, u32[]{:S(2)}, u32[]{:S(2)}) %all-to-all-start.2) | async-done | bytes 1835040 | tf_op jit(solution)/shard_map/all_to_all | solution.py:72
  186.7 0.3 convert_reduce_fusion
  187.0 0.9 copy-done.2
  187.9 0.3 fusion.36
  188.2 1.3 fusion.39
  189.5 0.0 all-gather.11.cloned.1.call-update
  189.5 0.1 copy.43
  189.6 0.1 maximum_bitcast_fusion.2
  189.7 6.1 %all-gather.3 = f32[4,2,33]{2,1,0:T(2,128)S(1)} all-gather(f32[1,2,33]{2,1,0:T(2,128)S(1)} %maximum_bitcast_fusion.2), channel_id=3, replica_groups=mesh['dp'=4,'cand'=32,'tensor'=4] {'tensor'}, dimensions={0}, use_global_device_ids=true | all-gather | bytes 1320 | tf_op jit(solution)/shard_map/all_gather | solution.py:83
  195.8 0.1 sub.37
  195.9 0.2 slice_reduce_fusion.1
  196.0 0.1 copy.45
  196.2 34.2 %all-gather.4 = f32[32,2,129]{2,1,0:T(2,128)S(1)} all-gather(f32[1,2,129]{2,1,0:T(2,128)S(1)} %maximum_bitcast_fusion.1), channel_id=4, replica_groups=mesh['dp'=4,'cand'=32,'tensor'=4] {'cand'}, dimensions={0}, use_global_device_ids=true | all-gather | bytes 34056 | tf_op jit(solution)/shard_map/all_gather | solution.py:86
  230.4 1.1 fusion.35
  231.5 0.1 copy.47
  231.6 0.1 slice_reduce_fusion
  231.8 6.6 %psum.14 = f32[2,129]{1,0:T(2,128)S(1)} all-reduce(f32[2,129]{1,0:T(2,128)S(1)} %pad_maximum_fusion), channel_id=1, replica_groups=mesh['dp'=4,'cand'=32,'tensor'=4] {'tensor'}, use_global_device_ids=true, to_apply=%region_11.12 | all-reduce | flops 258 | bytes 2064 | tf_op jit(solution)/shard_map/psum | solution.py:93
  238.4 0.1 slice_reduce_fusion.2
  238.5 0.2 dynamic_update_slice.3
  238.7 0.1 broadcast_multiply_fusion
  238.8 0.1 constant_dynamic-slice_fusion.1
  238.9 2.1 multiply_convert_fusion.1
  241.0 2.2 fusion.44
  243.2 0.4 fusion.48
  243.6 0.2 convolution_bitcast_fusion.1
  243.7 0.3 fusion.20
  244.1 0.8 copy.48
  244.8 9.0 %all-to-all-start.3 = ((f32[32,1,1024]{2,1,0:T(1,128)}), f32[32,1,1024]{2,1,0:T(1,128)S(1)}, u32[]{:S(2)}, u32[]{:S(2)}) async-start(f32[32,1,1024]{2,1,0:T(1,128)} %copy.48), calls=%async_computation.3 | async-start | bytes 262144 | tf_op jit(solution)/shard_map/all_to_all | solution.py:118
  253.8 5.7 %fusion.17 = bf16[2,128,896]{2,1,0:T(8,128)(2,1)} fusion(f32[2,128,896]{2,1,0:T(8,128)S(1)} %fusion.48, bf16[2,128,3584]{2,1,0:T(8,128)(2,1)S(1)} %copy-done.3, bf16[3584,896]{1,0:T(8,128)(2,1)} %all-gather.9.cloned.1.call-done, f32[2,128]{1,0:T(2,128)S(1)} %get-tuple-element.31), kind=kOutput, calls=%fused_computation.22 | convolution fusion | flops 1644855296 | bytes 9634816 | tf_op jit(solution)/shard_map/qcd,dh->qch/dot_general | solution.py:100
  259.5 10.2 %all-to-all-done.3 = f32[32,1,1024]{2,1,0:T(1,128)S(1)} async-done(((f32[32,1,1024]{2,1,0:T(1,128)}), f32[32,1,1024]{2,1,0:T(1,128)S(1)}, u32[]{:S(2)}, u32[]{:S(2)}) %all-to-all-start.3) | async-done | bytes 131104 | tf_op jit(solution)/shard_map/all_to_all | solution.py:118
  269.7 0.1 reduce_sum.134
  269.8 8.4 %psum.15 = f32[1,1024]{1,0:T(1,128)S(1)} all-reduce(f32[1,1024]{1,0:T(1,128)S(1)} %bitcast.87), channel_id=1, replica_groups=mesh['dp'=4,'cand'=32,'tensor'=4] {'dp'}, use_global_device_ids=true, to_apply=%region_14.15 | all-reduce | flops 1024 | bytes 8192 | tf_op jit(solution)/shard_map/psum | solution.py:120
  278.2 0.6 fusion.57
  278.8 30.8 %all-gather.5 = f32[32,1,896]{2,1,0:T(1,128)S(1)} all-gather(f32[1,1,896]{2,1,0:T(1,128)S(1)} %slice_bitcast_fusion.1), channel_id=1, replica_groups=mesh['dp'=4,'cand'=32,'tensor'=4] {'cand'}, dimensions={0}, use_global_device_ids=true | all-gather | bytes 118272 | tf_op jit(solution)/shard_map/all_gather | solution.py:121
  309.6 0.6 copy_bitcast_fusion
  (33 shorter events, 0.2 us)
Async XLA Ops:
  7.2 130.8 %copy-start = (bf16[16,3584]{1,0:T(8,128)(2,1)S(1)}, bf16[16,3584]{1,0:T(8,128)(2,1)}, u32[]{:S(2)}) copy-start(bf16[16,3584]{1,0:T(8,128)(2,1)} %param.14) | copy-start | bytes 344068
  7.2 143.6 %all-gather.9.cloned.1.call-start = ((), (), s32[]{:S(2)}) async-start(), calls=%async_computation.4 | async-start | bytes 6623232 | tf_op jit(solution)/shard_map/all_gather | solution.py:33
  9.6 26.5 %copy-start.6 = (bf16[2,128,1024]{2,1,0:T(8,128)(2,1)S(1)}, bf16[2,128,1024]{2,1,0:T(8,128)(2,1)}, u32[]{:S(2)}) copy-start(bf16[2,128,1024]{2,1,0:T(8,128)(2,1)} %param.17) | copy-start | bytes 1572868
  34.3 2.0 collective-permute-start
  36.3 6.3 %copy-start.4 = (bf16[2,128,896]{2,1,0:T(8,128)(2,1)S(1)}, bf16[2,128,896]{2,1,0:T(8,128)(2,1)}, u32[]{:S(2)}) copy-start(bf16[2,128,896]{2,1,0:T(8,128)(2,1)} %param.10) | copy-start | bytes 1376260
  36.3 6.3 %copy-start.8 = (bf16[896,16]{0,1:T(8,128)(2,1)S(1)}, bf16[896,16]{0,1:T(8,128)(2,1)}, u32[]{:S(2)}) copy-start(bf16[896,16]{0,1:T(8,128)(2,1)} %param.13) | copy-start | bytes 86020
  36.3 101.6 %copy-start.7 = (bf16[2,32,3584]{2,1,0:T(8,128)(2,1)S(1)}, bf16[2,32,3584]{2,1,0:T(8,128)(2,1)}, u32[]{:S(2)}) copy-start(bf16[2,32,3584]{2,1,0:T(8,128)(2,1)} %param.11) | copy-start | bytes 1376260
  38.3 98.9 %all-to-all-start.1 = ((f32[8,2,128]{2,1,0:T(2,128)}), f32[8,2,128]{2,1,0:T(2,128)S(1)}, u32[]{:S(2)}, u32[]{:S(2)}) async-start(f32[8,2,128]{2,1,0:T(2,128)} %bitcast.8), calls=%async_computation.1 | async-start | bytes 16384 | tf_op jit(solution)/shard_map/all_to_all | solution.py:61
  137.3 2.0 collective-permute-start.1
  156.9 29.8 %all-to-all-start.2 = ((bf16[4,2,32,3584]{3,2,1,0:T(8,128)(2,1)}), bf16[4,2,32,3584]{3,2,1,0:T(8,128)(2,1)S(1)}, u32[]{:S(2)}, u32[]{:S(2)}) async-start(bf16[4,2,32,3584]{3,2,1,0:T(8,128)(2,1)} %fusion.7), calls=%async_computation.2 | async-start | bytes 3670016 | tf_op jit(solution)/shard_map/all_to_all | solution.py:72
  163.7 77.3 %all-gather.11.cloned.1.call-start = ((), (), s32[]{:S(2)}) async-start(), calls=%async_computation.5 | async-start | bytes 2293760 | tf_op jit(solution)/shard_map/all_gather | solution.py:81
  186.7 1.2 copy-start.2
  187.9 42.5 %copy-start.1 = (f32[2,128,1024]{1,2,0:T(8,128)S(1)}, f32[2,128,1024]{1,2,0:T(8,128)}, u32[]{:S(2)}) copy-start(f32[2,128,1024]{1,2,0:T(8,128)} %get-tuple-element.14) | copy-start | bytes 3145732
  189.5 42.3 %copy-start.10 = (f32[2]{0:T(128)S(1)}, f32[2]{0:T(128)}, u32[]{:S(2)}) copy-start(f32[2]{0:T(128)} %param.19) | copy-start | bytes 28
  231.5 11.7 %copy-start.9 = (bf16[896,16]{0,1:T(8,128)(2,1)S(1)}, bf16[896,16]{0,1:T(8,128)(2,1)}, u32[]{:S(2)}) copy-start(bf16[896,16]{0,1:T(8,128)(2,1)} %param.13) | copy-start | bytes 86020
  238.9 4.7 %copy-start.5 = (bf16[2,128,896]{2,1,0:T(8,128)(2,1)S(1)}, bf16[2,128,896]{2,1,0:T(8,128)(2,1)}, u32[]{:S(2)}) copy-start(bf16[2,128,896]{2,1,0:T(8,128)(2,1)} %param.10) | copy-start | bytes 1376260
  241.0 2.7 copy-start.3
  244.8 24.9 %all-to-all-start.3 = ((f32[32,1,1024]{2,1,0:T(1,128)}), f32[32,1,1024]{2,1,0:T(1,128)S(1)}, u32[]{:S(2)}, u32[]{:S(2)}) async-start(f32[32,1,1024]{2,1,0:T(1,128)} %copy.48), calls=%async_computation.3 | async-start | bytes 262144 | tf_op jit(solution)/shard_map/all_to_all | solution.py:118
Sparse Core Ops, SparseCore 0:
  10.1 140.5 all-gather.8
  189.6 34.0 all-gather.10
where the time goes:
time: 318 us; the launch traced here: 317 us
  blocking collectives  204 us (64%)
  waiting for transfers between devices  44.7 us (14%)
  starting transfers between devices  22.4 us (7%)
  matrix products  16.3 us (5%)
  between operations  14.2 us (4%)
  other arithmetic  9.15 us (3%)
  local copies, waits for them, and re-layouts  6.21 us (2%)
    all_gather x1, blocking collectives, on_device(): low_all = lax.all_gather(low_terms, 'tensor', axis=0)  94.4 us
    all_gather x1, blocking collectives, on_device(): message = lax.all_gather(message, 'cand', axis=0)  34.2 us
    all_gather x1, blocking collectives, on_device(): flat = lax.all_gather(piece[:, :columns], 'cand', axis=0, tiled=True)  30.8 us
    all_to_all x1, blocking collectives, on_device(): lax.all_to_all(blocks, 'cand', 0, 0, axis_index_groups=groups, tiled=True)  23.6 us
    all_to_all x1, waiting for transfers between devices, on_device(): head_terms = lax.all_to_all(head_terms, 'tensor', 0, 0, tiled=True)  22.3 us
    all_gather x1, waiting for transfers between devices, on_device(): full_weight = lax.all_gather(out_weight, 'cand', axis=0, tiled=True)  11.5 us
    all_to_all x1, waiting for transfers between devices, on_device(): pieces = lax.all_to_all(flat, 'cand', 0, 0, tiled=True)  10.2 us
    all_to_all x1, starting transfers between devices, on_device(): pieces = lax.all_to_all(flat, 'cand', 0, 0, tiled=True)  9 us
  transfers between devices with their start and end apart: 7, of which 3 were waited for; matrix products, arithmetic and copies ran while one was open for 6% of the time, Pallas kernels for 0%

commit v1 on v0

--- a/solution.py
+++ b/solution.py
@@ -7,6 +7,7 @@
 epsilon = 1e-06
 F32 = jnp.float32
 BF16 = jnp.bfloat16
+wait_quarters_for = lambda axis_key, xx: jnp.sum(lax.all_gather(xx, axis_key), 0)
 
 
 def on_device(
@@ -117,7 +118,7 @@
     flat = jnp.concatenate([flat, jnp.broadcast_to(slots, (flat.shape[0], 128))], axis=1)
     pieces = lax.all_to_all(flat, "cand", 0, 0, tiled=True)
     piece = jnp.sum(pieces.reshape(cand_count, -1, flat.shape[1]), axis=0)
-    piece = lax.psum(piece, "dp")
+    piece = wait_quarters_for("dp", piece)
     flat = lax.all_gather(piece[:, :columns], "cand", axis=0, tiled=True)
     rank = adapter_down.shape[1]
     down_grad = flat[:rank].T

time: 318 us -> 320 us (level)
    all_gather x0 -> x1, blocking collectives: none -> 9.4 us  [lax.all_gather(xx, axis_key)]
    psum x1 -> x0, blocking collectives: 8.39 us -> none  [on_device(): piece = lax.psum(piece, 'dp')]
  transfers between devices with their start and end apart: 7 -> 7, of which waited for: 3 -> 3; matrix products, arithmetic and copies ran while one was open for 6% -> 5% of each run, Pallas kernels for 0% -> 0%
where the time goes in v1:
time: 320 us; the launch traced here: 319 us
  blocking collectives  206 us (64%)
  waiting for transfers between devices  44.5 us (14%)
  starting transfers between devices  22.5 us (7%)
  matrix products  16.3 us (5%)
  between operations  14.3 us (4%)
  other arithmetic  9.17 us (3%)
  local copies, waits for them, and re-layouts  6.21 us (2%)
    all_gather x1, blocking collectives, on_device(): low_all = lax.all_gather(low_terms, 'tensor', axis=0)  94.4 us
    all_gather x1, blocking collectives, on_device(): message = lax.all_gather(message, 'cand', axis=0)  34.3 us
    all_gather x1, blocking collectives, on_device(): flat = lax.all_gather(piece[:, :columns], 'cand', axis=0, tiled=True)  31.7 us
    all_to_all x1, blocking collectives, on_device(): lax.all_to_all(blocks, 'cand', 0, 0, axis_index_groups=groups, tiled=True)  23.6 us
    all_to_all x1, waiting for transfers between devices, on_device(): head_terms = lax.all_to_all(head_terms, 'tensor', 0, 0, tiled=True)  22.2 us
    all_gather x1, waiting for transfers between devices, on_device(): full_weight = lax.all_gather(out_weight, 'cand', axis=0, tiled=True)  11.4 us
    all_to_all x1, waiting for transfers between devices, on_device(): pieces = lax.all_to_all(flat, 'cand', 0, 0, tiled=True)  10.2 us
    all_gather x1, blocking collectives, lax.all_gather(xx, axis_key)  9.4 us
  transfers between devices with their start and end apart: 7, of which 3 were waited for; matrix products, arithmetic and copies ran while one was open for 5% of the time, Pallas kernels for 0%

profile of v1, /device:TPU:1, one launch (start us, length us, event | category | flops | bytes accessed | tf_op | source)
XLA Modules:
  0.0 319.0 jit_solution(451481984941035531)
XLA Ops:
  7.2 0.0 copy-start
  7.2 0.0 all-gather.10.cloned.1.call-start
  7.2 0.7 all-gather.10.cloned.1.call-update
  7.9 1.5 copy.49
  9.5 0.1 convert_element_type.65
  9.6 0.0 copy-start.6
  9.6 0.3 copy.51
  9.8 23.6 %all_to_all.24 = bf16[8,2,128,128]{2,3,1,0:T(8,128)(2,1)S(1)} all-to-all(bf16[8,2,128,128]{2,3,1,0:T(8,128)(2,1)S(1)} %copy.51), channel_id=1, replica_groups={{0,4,8,12,16,20,24,28},{32,36,40,44,48,52,56,60},{64,68,72,76,80,84,88,..., dimensions={0} | all-to-all | bytes 1048576 | tf_op jit(solution)/shard_map/all_to_all | solution.py:58
  33.5 0.8 copy.52
  34.3 1.7 collective-permute-start
  36.0 0.3 copy.53
  36.3 0.0 copy-start.4
  36.3 0.0 copy-start.8
  36.3 0.0 copy-start.7
  36.3 0.0 collective-permute-done
  36.3 2.0 fusion.23
  38.3 4.3 %all-to-all-start.1 = ((f32[8,2,128]{2,1,0:T(2,128)}), f32[8,2,128]{2,1,0:T(2,128)S(1)}, u32[]{:S(2)}, u32[]{:S(2)}) async-start(f32[8,2,128]{2,1,0:T(2,128)} %bitcast.8), calls=%async_computation.1 | async-start | bytes 16384 | tf_op jit(solution)/shard_map/all_to_all | solution.py:62
  42.6 0.0 copy-done.4
  42.6 0.2 convolution_convert_fusion
  42.8 94.4 %all-gather = bf16[8,128,16]{1,2,0:T(8,128)(2,1)S(1)} all-gather(bf16[2,128,16]{1,2,0:T(8,128)(2,1)S(1)} %convolution_convert_fusion), channel_id=2, replica_groups=mesh['dp'=4,'cand'=32,'tensor'=4] {'tensor'}, dimensions={0}, use_global_device_ids=true | all-gather | bytes 40960 | tf_op jit(solution)/shard_map/all_gather | solution.py:38
  137.2 0.0 all-to-all-done.1
  137.2 0.7 collective-permute-start.1
  137.9 1.3 fusion.10
  139.2 0.0 collective-permute-done.1
  139.2 11.4 %all-gather.10.cloned.1.call-done = bf16[3584,896]{1,0:T(8,128)(2,1)} async-done(((bf16[112,896]{1,0:T(8,128)(2,1)}), bf16[3584,896]{1,0:T(8,128)(2,1)}) %all-gather.10.cloned.1.call-update) | async-done | bytes 6422544 | tf_op jit(solution)/shard_map/all_gather | solution.py:34
  150.6 6.2 %fusion.7 = bf16[4,2,32,3584]{3,2,1,0:T(8,128)(2,1)} fusion(bf16[3584,896]{1,0:T(8,128)(2,1)} %all-gather.10.cloned.1.call-done, bf16[2,4,32,896]{3,2,1,0:T(8,128)(2,1)S(1)} %bitcast.85), kind=kOutput, calls=%fused_computation.5 | convolution fusion | flops 1645084672 | bytes 8716288 | tf_op jit(solution)/shard_map/tqch,dh->tqcd/dot_general | solution.py:70
  156.8 6.8 %all-to-all-start.2 = ((bf16[4,2,32,3584]{3,2,1,0:T(8,128)(2,1)}), bf16[4,2,32,3584]{3,2,1,0:T(8,128)(2,1)S(1)}, u32[]{:S(2)}, u32[]{:S(2)}) async-start(bf16[4,2,32,3584]{3,2,1,0:T(8,128)(2,1)} %fusion.7), calls=%async_computation.2 | async-start | bytes 3670016 | tf_op jit(solution)/shard_map/all_to_all | solution.py:73
  163.6 0.7 mul.141
  164.4 22.2 %all-to-all-done.2 = bf16[4,2,32,3584]{3,2,1,0:T(8,128)(2,1)S(1)} async-done(((bf16[4,2,32,3584]{3,2,1,0:T(8,128)(2,1)}), bf16[4,2,32,3584]{3,2,1,0:T(8,128)(2,1)S(1)}, u32[]{:S(2)}, u32[]{:S(2)}) %all-to-all-start.2) | async-done | bytes 1835040 | tf_op jit(solution)/shard_map/all_to_all | solution.py:73
  186.6 0.3 convert_reduce_fusion
  186.9 0.9 copy-done.2
  187.8 0.3 fusion.36
  188.1 1.3 fusion.39
  189.3 0.0 all-gather.12.cloned.1.call-update
  189.4 0.1 copy.56
  189.5 0.1 maximum_bitcast_fusion.2
  189.5 6.1 %all-gather.4 = f32[4,2,33]{2,1,0:T(2,128)S(1)} all-gather(f32[1,2,33]{2,1,0:T(2,128)S(1)} %maximum_bitcast_fusion.2), channel_id=3, replica_groups=mesh['dp'=4,'cand'=32,'tensor'=4] {'tensor'}, dimensions={0}, use_global_device_ids=true | all-gather | bytes 1320 | tf_op jit(solution)/shard_map/all_gather | solution.py:84
  195.7 0.1 sub.37
  195.7 0.2 slice_reduce_fusion.1
  195.9 0.1 copy.58
  196.0 34.3 %all-gather.5 = f32[32,2,129]{2,1,0:T(2,128)S(1)} all-gather(f32[1,2,129]{2,1,0:T(2,128)S(1)} %maximum_bitcast_fusion.1), channel_id=4, replica_groups=mesh['dp'=4,'cand'=32,'tensor'=4] {'cand'}, dimensions={0}, use_global_device_ids=true | all-gather | bytes 34056 | tf_op jit(solution)/shard_map/all_gather | solution.py:87
  230.4 1.1 fusion.35
  231.5 0.1 copy.60
  231.6 0.1 slice_reduce_fusion
  231.8 6.6 %psum.7 = f32[2,129]{1,0:T(2,128)S(1)} all-reduce(f32[2,129]{1,0:T(2,128)S(1)} %pad_maximum_fusion), channel_id=1, replica_groups=mesh['dp'=4,'cand'=32,'tensor'=4] {'tensor'}, use_global_device_ids=true, to_apply=%region_11.12 | all-reduce | flops 258 | bytes 2064 | tf_op jit(solution)/shard_map/psum | solution.py:94
  238.4 0.1 slice_reduce_fusion.2
  238.5 0.2 dynamic_update_slice.3
  238.7 0.1 broadcast_multiply_fusion
  238.8 0.1 constant_dynamic-slice_fusion.1
  238.9 2.1 multiply_convert_fusion.1
  241.0 2.2 fusion.44
  243.2 0.0 copy-done.9
  243.2 0.4 fusion.48
  243.6 0.2 convolution_bitcast_fusion.1
  243.7 0.3 fusion.20
  244.0 0.8 copy.61
  244.8 9.0 %all-to-all-start.3 = ((f32[32,1,1024]{2,1,0:T(1,128)}), f32[32,1,1024]{2,1,0:T(1,128)S(1)}, u32[]{:S(2)}, u32[]{:S(2)}) async-start(f32[32,1,1024]{2,1,0:T(1,128)} %copy.61), calls=%async_computation.3 | async-start | bytes 262144 | tf_op jit(solution)/shard_map/all_to_all | solution.py:119
  253.8 5.7 %fusion.17 = bf16[2,128,896]{2,1,0:T(8,128)(2,1)} fusion(f32[2,128,896]{2,1,0:T(8,128)S(1)} %fusion.48, bf16[2,128,3584]{2,1,0:T(8,128)(2,1)S(1)} %copy-done.3, bf16[3584,896]{1,0:T(8,128)(2,1)} %all-gather.10.cloned.1.call-done, f32[2,128]{1,0:T(2,128)S(1)} %get-tuple-element.31), kind=kOutput, calls=%fused_computation.22 | convolution fusion | flops 1644855296 | bytes 9634816 | tf_op jit(solution)/shard_map/qcd,dh->qch/dot_general | solution.py:101
  259.5 10.2 %all-to-all-done.3 = f32[32,1,1024]{2,1,0:T(1,128)S(1)} async-done(((f32[32,1,1024]{2,1,0:T(1,128)}), f32[32,1,1024]{2,1,0:T(1,128)S(1)}, u32[]{:S(2)}, u32[]{:S(2)}) %all-to-all-start.3) | async-done | bytes 131104 | tf_op jit(solution)/shard_map/all_to_all | solution.py:119
  269.7 0.1 reduce_sum.143
  269.8 9.4 %all-gather.3 = f32[4096]{0:T(1024)S(1)} all-gather(f32[1024]{0:T(1024)S(1)} %reduce_sum.143), channel_id=5, replica_groups=mesh['dp'=4,'cand'=32,'tensor'=4] {'dp'}, dimensions={0}, use_global_device_ids=true | all-gather | bytes 20480 | tf_op jit(solution)/shard_map/all_gather | solution.py:10
  279.2 0.6 fusion.57
  279.8 31.7 %all-gather.6 = f32[32,1,896]{2,1,0:T(1,128)S(1)} all-gather(f32[1,1,896]{2,1,0:T(1,128)S(1)} %slice_bitcast_fusion.1), channel_id=1, replica_groups=mesh['dp'=4,'cand'=32,'tensor'=4] {'cand'}, dimensions={0}, use_global_device_ids=true | all-gather | bytes 118272 | tf_op jit(solution)/shard_map/all_gather | solution.py:122
  311.5 0.6 copy_bitcast_fusion
  (35 shorter events, 0.2 us)
Async XLA Ops:
  7.2 130.7 %copy-start = (bf16[16,3584]{1,0:T(8,128)(2,1)S(1)}, bf16[16,3584]{1,0:T(8,128)(2,1)}, u32[]{:S(2)}) copy-start(bf16[16,3584]{1,0:T(8,128)(2,1)} %param.14) | copy-start | bytes 344068
  7.2 143.4 %all-gather.10.cloned.1.call-start = ((), (), s32[]{:S(2)}) async-start(), calls=%async_computation.4 | async-start | bytes 6623232 | tf_op jit(solution)/shard_map/all_gather | solution.py:34
  9.6 26.4 %copy-start.6 = (bf16[2,128,1024]{2,1,0:T(8,128)(2,1)S(1)}, bf16[2,128,1024]{2,1,0:T(8,128)(2,1)}, u32[]{:S(2)}) copy-start(bf16[2,128,1024]{2,1,0:T(8,128)(2,1)} %param.17) | copy-start | bytes 1572868
  34.3 2.0 collective-permute-start
  36.3 6.3 %copy-start.4 = (bf16[2,128,896]{2,1,0:T(8,128)(2,1)S(1)}, bf16[2,128,896]{2,1,0:T(8,128)(2,1)}, u32[]{:S(2)}) copy-start(bf16[2,128,896]{2,1,0:T(8,128)(2,1)} %param.10) | copy-start | bytes 1376260
  36.3 6.3 %copy-start.8 = (bf16[896,16]{0,1:T(8,128)(2,1)S(1)}, bf16[896,16]{0,1:T(8,128)(2,1)}, u32[]{:S(2)}) copy-start(bf16[896,16]{0,1:T(8,128)(2,1)} %param.13) | copy-start | bytes 86020
  36.3 101.6 %copy-start.7 = (bf16[2,32,3584]{2,1,0:T(8,128)(2,1)S(1)}, bf16[2,32,3584]{2,1,0:T(8,128)(2,1)}, u32[]{:S(2)}) copy-start(bf16[2,32,3584]{2,1,0:T(8,128)(2,1)} %param.11) | copy-start | bytes 1376260
  38.3 98.9 %all-to-all-start.1 = ((f32[8,2,128]{2,1,0:T(2,128)}), f32[8,2,128]{2,1,0:T(2,128)S(1)}, u32[]{:S(2)}, u32[]{:S(2)}) async-start(f32[8,2,128]{2,1,0:T(2,128)} %bitcast.8), calls=%async_computation.1 | async-start | bytes 16384 | tf_op jit(solution)/shard_map/all_to_all | solution.py:62
  137.2 2.0 collective-permute-start.1
  156.8 29.8 %all-to-all-start.2 = ((bf16[4,2,32,3584]{3,2,1,0:T(8,128)(2,1)}), bf16[4,2,32,3584]{3,2,1,0:T(8,128)(2,1)S(1)}, u32[]{:S(2)}, u32[]{:S(2)}) async-start(bf16[4,2,32,3584]{3,2,1,0:T(8,128)(2,1)} %fusion.7), calls=%async_computation.2 | async-start | bytes 3670016 | tf_op jit(solution)/shard_map/all_to_all | solution.py:73
  163.6 77.4 %all-gather.12.cloned.1.call-start = ((), (), s32[]{:S(2)}) async-start(), calls=%async_computation.5 | async-start | bytes 2293760 | tf_op jit(solution)/shard_map/all_gather | solution.py:82
  186.6 1.2 copy-start.2
  187.8 42.6 %copy-start.1 = (f32[2,128,1024]{1,2,0:T(8,128)S(1)}, f32[2,128,1024]{1,2,0:T(8,128)}, u32[]{:S(2)}) copy-start(f32[2,128,1024]{1,2,0:T(8,128)} %get-tuple-element.14) | copy-start | bytes 3145732
  189.3 42.4 %copy-start.10 = (f32[2]{0:T(128)S(1)}, f32[2]{0:T(128)}, u32[]{:S(2)}) copy-start(f32[2]{0:T(128)} %param.19) | copy-start | bytes 28
  231.5 11.7 %copy-start.9 = (bf16[896,16]{0,1:T(8,128)(2,1)S(1)}, bf16[896,16]{0,1:T(8,128)(2,1)}, u32[]{:S(2)}) copy-start(bf16[896,16]{0,1:T(8,128)(2,1)} %param.13) | copy-start | bytes 86020
  238.9 4.7 %copy-start.5 = (bf16[2,128,896]{2,1,0:T(8,128)(2,1)S(1)}, bf16[2,128,896]{2,1,0:T(8,128)(2,1)}, u32[]{:S(2)}) copy-start(bf16[2,128,896]{2,1,0:T(8,128)(2,1)} %param.10) | copy-start | bytes 1376260
  241.0 2.7 copy-start.3
  244.8 24.9 %all-to-all-start.3 = ((f32[32,1,1024]{2,1,0:T(1,128)}), f32[32,1,1024]{2,1,0:T(1,128)S(1)}, u32[]{:S(2)}, u32[]{:S(2)}) async-start(f32[32,1,1024]{2,1,0:T(1,128)} %copy.61), calls=%async_computation.3 | async-start | bytes 262144 | tf_op jit(solution)/shard_map/all_to_all | solution.py:119
Sparse Core Ops, SparseCore 0:
  10.1 140.4 all-gather.9
  189.5 34.1 all-gather.11
